TPU v7x, 32 devices: a whole 2x2x4 slice. The times are simulated.
32 devices in a mesh: pair: 8 (over y, x, core), ints: 4 (over z).
Axes of the slice: x: 2, y: 2, z: 4, core: 2. Of those that a mesh axis runs over, the one named last changes fastest.
Arguments:
- t_amps: bfloat16 [32, 8, 4096], P('pair', None, 'ints'), may hold values from -6 to 6
- block_mask: int32 [32, 8, 64], P('pair', None, 'ints'), may hold values 0 or 1
- factors: bfloat16 [8, 64, 64, 128], P('pair', 'ints'), may hold values from -0.75 to 0.75
- links: int32 [8, 64, 32], P('pair', 'ints'), may hold values from 0 to 63, as said below
- link_counts: int32 [8, 64], P('pair', 'ints'), may hold values from 8 to 32, as said below
Outputs:
- ladder: bfloat16 [32, 8, 4096], P('pair', None, 'ints')
Inputs may be any that keep to these rules, and one draw needn't show every extreme that they name: `links`: the 32 slots of a tile name distinct tiles of its own block; only the first link_counts slots are used. `link_counts`: in every block, tile 0 uses all 32 slots.
All inputs are finite; a program needn't handle non-finite values. No bound on the sum of `block_mask` on one device may be relied on, other than what follows from the above.
Results may differ from a plain program's by a relative error of at most 0.008.
Values may be sent and summed in bfloat16 or wider, within the bound.
A program may use at most 128 MiB of HBM per device.

v0:
```python
import jax
import jax.numpy as jnp
from jax import lax
from jax.sharding import PartitionSpec as P


def split_high(values):
    high = values.astype(jnp.bfloat16)
    rest = (values - high.astype(jnp.float32)).astype(jnp.bfloat16)
    return (high, rest)


def tile_ladder(all_f, all_t, own_f, link_rows, count_rows):
    slots = jnp.arange(link_rows.shape[-1], dtype=jnp.int32)
    npairs = all_t.shape[0]
    tile = own_f.shape[1]
    amp_tiles = all_t.reshape(npairs, all_f.shape[0], tile)

    def one_tile(inputs):
        own, index_row, count = inputs
        near_f = jnp.take(all_f, index_row, axis=0)
        near_t = jnp.take(amp_tiles, index_row, axis=1)
        used = (slots < count).astype(jnp.float32)
        blocks = jnp.einsum("xq,kyq->kxy", own, near_f, preferred_element_type=jnp.float32)
        blocks = blocks * used[:, None, None]
        high, rest = split_high(blocks)
        first = jnp.einsum("kxy,pky->px", high, near_t, preferred_element_type=jnp.float32)
        second = jnp.einsum("kxy,pky->px", rest, near_t, preferred_element_type=jnp.float32)
        return first + second

    stacked = lax.map(one_tile, (own_f, link_rows, count_rows))
    return jnp.transpose(stacked, (1, 0, 2)).reshape(npairs, own_f.shape[0] * tile)


def body(t_amps, block_mask, factors, links, link_counts):
    own_f = factors[0]
    link_rows = links[0]
    count_rows = link_counts[0]
    tile_count = own_f.shape[0]
    tile = own_f.shape[1]
    pair_dev, nblocks, width = t_amps.shape
    shaped = t_amps.reshape(pair_dev, nblocks, tile_count, tile)
    masked = (shaped * block_mask[:, :, :, None].astype(t_amps.dtype)).reshape(
        pair_dev, nblocks, width
    )
    local = lax.all_to_all(masked, "pair", split_axis=1, concat_axis=0, tiled=True)[:, 0, :]
    all_f, all_t = (
        lax.all_gather(own_f, "ints", axis=0, tiled=True),
        lax.all_gather(local, "ints", axis=1, tiled=True),
    )
    result = tile_ladder(all_f, all_t, own_f, link_rows, count_rows)
    rounded = result.astype(jnp.bfloat16)[:, None, :]
    return lax.all_to_all(rounded, "pair", split_axis=0, concat_axis=1, tiled=True)


def solution(mesh):
    placed = (
        P("pair", None, "ints"),
        P("pair", None, "ints"),
        P("pair", "ints", None, None),
        P("pair", "ints", None),
        P("pair", "ints"),
    )
    return jax.shard_map(
        body, mesh=mesh, in_specs=placed, out_specs=P("pair", None, "ints"), check_vma=False
    )
```

profile of v0, /device:TPU:0, one launch (start us, length us, event | category | flops | bytes accessed | tf_op | source)
XLA Modules:
  0.0 173.8 jit_solution(7210912905600619136)
XLA Ops:
  6.5 0.7 all-gather.3.cloned.1.call-update
  9.0 5.2 %all-to-all-start = ((bf16[4,8,1024]{2,0,1:T(4,128)(2,1)}), bf16[4,8,1024]{2,0,1:T(4,128)(2,1)S(1)}, u32[]{:S(2)}, u32[]{:S(2)}) async-start(bf16[4,8,1024]{2,0,1:T(4,128)(2,1)} %copy.27), calls=%async_computation | async-start | bytes 131072 | tf_op jit(solution)/shard_map/all_to_all | solution.py:46
  14.2 5.0 %all-to-all-done = bf16[4,8,1024]{2,0,1:T(4,128)(2,1)S(1)} async-done(((bf16[4,8,1024]{2,0,1:T(4,128)(2,1)}), bf16[4,8,1024]{2,0,1:T(4,128)(2,1)S(1)}, u32[]{:S(2)}, u32[]{:S(2)}) %all-to-all-start) | async-done | bytes 65568 | tf_op jit(solution)/shard_map/all_to_all | solution.py:46
  19.2 16.7 %all_gather.6 = bf16[32,4096]{1,0:T(8,128)(2,1)S(1)} all-gather(bf16[32,1024]{1,0:T(8,128)(2,1)S(1)} %squeeze.27), channel_id=1, replica_groups=mesh['pair'=8,'ints'=4] {'ints'}, dimensions={1}, use_global_device_ids=true | all-gather | bytes 327680 | tf_op jit(solution)/shard_map/all_gather | solution.py:49
  36.8 7.0 %all-gather.3.cloned.1.call-done = bf16[1,64,64,128]{3,2,0,1:T(8,128)(2,1)} async-done(((bf16[1,16,64,128]{3,2,0,1:T(8,128)(2,1)}), bf16[1,64,64,128]{3,2,0,1:T(8,128)(2,1)}) %all-gather.3.cloned.1.call-update) | async-done | bytes 1048592 | tf_op jit(solution)/shard_map/all_gather | solution.py:48
  44.5 110.9 %while.11 = (s32[]{:T(128)}, bf16[16,32,64]{2,1,0:T(8,128)(2,1)S(1)}, s32[16,32]{1,0:T(8,128)}, bf16[32,64,64]{2,0,1:T(8,128)(2,1)S(1)}, bf16[64,64,128]{2,1,0:T...) while((s32[]{:T(128)}, bf16[16,32,64]{2,1,0:T(8,128)(2,1)S(1)}, ...), condition=%wide.region_1.2_spmd.clone, body=%wide.region_0.1_spmd.clone.sunk | while | flops 51514720 | bytes 4389073 | solution.py:31
  45.1 1.3 compare_convert_fusion.2
  46.4 0.7 fusion.33
  47.1 1.9 %gather_fusion = bf16[32,64,128]{2,1,0:T(8,128)(2,1)S(1)} fusion(bf16[64,64,128]{2,1,0:T(8,128)(2,1)} %get-tuple-element.168, s32[1024]{0:T(1024)S(1)} %pad_clamp_fusion.2), kind=kCustom, calls=%fused_computation.1.clone.clone.1 | custom fusion | bytes 1048704 | tf_op jit(solution)/shard_map/while/body/eval_jaxpr/jit(_take)/gather | solution.py:21
  49.0 1.1 fusion.34
  52.0 1.3 compare_convert_fusion.2
  54.1 1.9 %gather_fusion = bf16[32,64,128]{2,1,0:T(8,128)(2,1)S(1)} fusion(bf16[64,64,128]{2,1,0:T(8,128)(2,1)} %get-tuple-element.168, s32[1024]{0:T(1024)S(1)} %pad_clamp_fusion.2), kind=kCustom, calls=%fused_computation.1.clone.clone.1 | custom fusion | bytes 1048704 | tf_op jit(solution)/shard_map/while/body/eval_jaxpr/jit(_take)/gather | solution.py:21
  55.9 1.1 fusion.34
  59.0 1.3 compare_convert_fusion.2
  61.0 1.9 %gather_fusion = bf16[32,64,128]{2,1,0:T(8,128)(2,1)S(1)} fusion(bf16[64,64,128]{2,1,0:T(8,128)(2,1)} %get-tuple-element.168, s32[1024]{0:T(1024)S(1)} %pad_clamp_fusion.2), kind=kCustom, calls=%fused_computation.1.clone.clone.1 | custom fusion | bytes 1048704 | tf_op jit(solution)/shard_map/while/body/eval_jaxpr/jit(_take)/gather | solution.py:21
  62.9 1.1 fusion.34
  65.9 1.3 compare_convert_fusion.2
  67.9 1.9 %gather_fusion = bf16[32,64,128]{2,1,0:T(8,128)(2,1)S(1)} fusion(bf16[64,64,128]{2,1,0:T(8,128)(2,1)} %get-tuple-element.168, s32[1024]{0:T(1024)S(1)} %pad_clamp_fusion.2), kind=kCustom, calls=%fused_computation.1.clone.clone.1 | custom fusion | bytes 1048704 | tf_op jit(solution)/shard_map/while/body/eval_jaxpr/jit(_take)/gather | solution.py:21
  69.8 1.1 fusion.34
  72.8 1.3 compare_convert_fusion.2
  74.2 0.7 fusion.33
  74.9 1.9 %gather_fusion = bf16[32,64,128]{2,1,0:T(8,128)(2,1)S(1)} fusion(bf16[64,64,128]{2,1,0:T(8,128)(2,1)} %get-tuple-element.168, s32[1024]{0:T(1024)S(1)} %pad_clamp_fusion.2), kind=kCustom, calls=%fused_computation.1.clone.clone.1 | custom fusion | bytes 1048704 | tf_op jit(solution)/shard_map/while/body/eval_jaxpr/jit(_take)/gather | solution.py:21
  76.7 1.1 fusion.34
  79.7 1.3 compare_convert_fusion.2
  81.8 1.9 %gather_fusion = bf16[32,64,128]{2,1,0:T(8,128)(2,1)S(1)} fusion(bf16[64,64,128]{2,1,0:T(8,128)(2,1)} %get-tuple-element.168, s32[1024]{0:T(1024)S(1)} %pad_clamp_fusion.2), kind=kCustom, calls=%fused_computation.1.clone.clone.1 | custom fusion | bytes 1048704 | tf_op jit(solution)/shard_map/while/body/eval_jaxpr/jit(_take)/gather | solution.py:21
  83.7 1.1 fusion.34
  86.7 1.3 compare_convert_fusion.2
  88.7 1.9 %gather_fusion = bf16[32,64,128]{2,1,0:T(8,128)(2,1)S(1)} fusion(bf16[64,64,128]{2,1,0:T(8,128)(2,1)} %get-tuple-element.168, s32[1024]{0:T(1024)S(1)} %pad_clamp_fusion.2), kind=kCustom, calls=%fused_computation.1.clone.clone.1 | custom fusion | bytes 1048704 | tf_op jit(solution)/shard_map/while/body/eval_jaxpr/jit(_take)/gather | solution.py:21
  90.6 1.1 fusion.34
  93.6 1.3 compare_convert_fusion.2
  94.9 0.7 fusion.33
  95.6 1.9 %gather_fusion = bf16[32,64,128]{2,1,0:T(8,128)(2,1)S(1)} fusion(bf16[64,64,128]{2,1,0:T(8,128)(2,1)} %get-tuple-element.168, s32[1024]{0:T(1024)S(1)} %pad_clamp_fusion.2), kind=kCustom, calls=%fused_computation.1.clone.clone.1 | custom fusion | bytes 1048704 | tf_op jit(solution)/shard_map/while/body/eval_jaxpr/jit(_take)/gather | solution.py:21
  97.5 1.1 fusion.34
  100.5 1.3 compare_convert_fusion.2
  101.9 0.7 fusion.33
  102.6 1.9 %gather_fusion = bf16[32,64,128]{2,1,0:T(8,128)(2,1)S(1)} fusion(bf16[64,64,128]{2,1,0:T(8,128)(2,1)} %get-tuple-element.168, s32[1024]{0:T(1024)S(1)} %pad_clamp_fusion.2), kind=kCustom, calls=%fused_computation.1.clone.clone.1 | custom fusion | bytes 1048704 | tf_op jit(solution)/shard_map/while/body/eval_jaxpr/jit(_take)/gather | solution.py:21
  104.5 1.1 fusion.34
  107.5 1.3 compare_convert_fusion.2
  108.8 0.7 fusion.33
  109.5 1.9 %gather_fusion = bf16[32,64,128]{2,1,0:T(8,128)(2,1)S(1)} fusion(bf16[64,64,128]{2,1,0:T(8,128)(2,1)} %get-tuple-element.168, s32[1024]{0:T(1024)S(1)} %pad_clamp_fusion.2), kind=kCustom, calls=%fused_computation.1.clone.clone.1 | custom fusion | bytes 1048704 | tf_op jit(solution)/shard_map/while/body/eval_jaxpr/jit(_take)/gather | solution.py:21
  111.4 1.1 fusion.34
  114.4 1.3 compare_convert_fusion.2
  115.7 0.7 fusion.33
  116.4 1.9 %gather_fusion = bf16[32,64,128]{2,1,0:T(8,128)(2,1)S(1)} fusion(bf16[64,64,128]{2,1,0:T(8,128)(2,1)} %get-tuple-element.168, s32[1024]{0:T(1024)S(1)} %pad_clamp_fusion.2), kind=kCustom, calls=%fused_computation.1.clone.clone.1 | custom fusion | bytes 1048704 | tf_op jit(solution)/shard_map/while/body/eval_jaxpr/jit(_take)/gather | solution.py:21
  118.3 1.1 fusion.34
  121.3 1.3 compare_convert_fusion.2
  122.7 0.7 fusion.33
  123.4 1.9 %gather_fusion = bf16[32,64,128]{2,1,0:T(8,128)(2,1)S(1)} fusion(bf16[64,64,128]{2,1,0:T(8,128)(2,1)} %get-tuple-element.168, s32[1024]{0:T(1024)S(1)} %pad_clamp_fusion.2), kind=kCustom, calls=%fused_computation.1.clone.clone.1 | custom fusion | bytes 1048704 | tf_op jit(solution)/shard_map/while/body/eval_jaxpr/jit(_take)/gather | solution.py:21
  125.2 1.1 fusion.34
  128.2 1.3 compare_convert_fusion.2
  129.6 0.7 fusion.33
  130.3 1.9 %gather_fusion = bf16[32,64,128]{2,1,0:T(8,128)(2,1)S(1)} fusion(bf16[64,64,128]{2,1,0:T(8,128)(2,1)} %get-tuple-element.168, s32[1024]{0:T(1024)S(1)} %pad_clamp_fusion.2), kind=kCustom, calls=%fused_computation.1.clone.clone.1 | custom fusion | bytes 1048704 | tf_op jit(solution)/shard_map/while/body/eval_jaxpr/jit(_take)/gather | solution.py:21
  132.2 1.1 fusion.34
  135.2 1.3 compare_convert_fusion.2
  137.2 1.9 %gather_fusion = bf16[32,64,128]{2,1,0:T(8,128)(2,1)S(1)} fusion(bf16[64,64,128]{2,1,0:T(8,128)(2,1)} %get-tuple-element.168, s32[1024]{0:T(1024)S(1)} %pad_clamp_fusion.2), kind=kCustom, calls=%fused_computation.1.clone.clone.1 | custom fusion | bytes 1048704 | tf_op jit(solution)/shard_map/while/body/eval_jaxpr/jit(_take)/gather | solution.py:21
  139.1 1.1 fusion.34
  142.1 1.3 compare_convert_fusion.2
  144.2 1.9 %gather_fusion = bf16[32,64,128]{2,1,0:T(8,128)(2,1)S(1)} fusion(bf16[64,64,128]{2,1,0:T(8,128)(2,1)} %get-tuple-element.168, s32[1024]{0:T(1024)S(1)} %pad_clamp_fusion.2), kind=kCustom, calls=%fused_computation.1.clone.clone.1 | custom fusion | bytes 1048704 | tf_op jit(solution)/shard_map/while/body/eval_jaxpr/jit(_take)/gather | solution.py:21
  146.0 1.1 fusion.34
  149.0 1.3 compare_convert_fusion.2
  151.1 1.9 %gather_fusion = bf16[32,64,128]{2,1,0:T(8,128)(2,1)S(1)} fusion(bf16[64,64,128]{2,1,0:T(8,128)(2,1)} %get-tuple-element.168, s32[1024]{0:T(1024)S(1)} %pad_clamp_fusion.2), kind=kCustom, calls=%fused_computation.1.clone.clone.1 | custom fusion | bytes 1048704 | tf_op jit(solution)/shard_map/while/body/eval_jaxpr/jit(_take)/gather | solution.py:21
  153.0 1.1 fusion.34
  156.1 1.0 reduce.1
  157.1 8.7 %all_to_all.33 = bf16[8,2,2048]{2,1,0:T(2,128)(2,1)S(1)} all-to-all(bf16[8,2,2048]{2,1,0:T(2,128)(2,1)S(1)} %reshape.86), channel_id=1, replica_groups=mesh['pair'=8,'ints'=4] {'pair'}, dimensions={0} | all-to-all | bytes 131072 | tf_op jit(solution)/shard_map/all_to_all | solution.py:53
  (112 shorter events, 41.0 us)
Async XLA Ops:
  6.5 37.3 %all-gather.3.cloned.1.call-start = ((), (), s32[]{:S(2)}) async-start(), calls=%async_computation.2 | async-start | bytes 1310720 | tf_op jit(solution)/shard_map/all_gather | solution.py:48
  6.5 0.7 copy-start.1
  7.4 0.8 copy-start
  9.0 10.2 %all-to-all-start = ((bf16[4,8,1024]{2,0,1:T(4,128)(2,1)}), bf16[4,8,1024]{2,0,1:T(4,128)(2,1)S(1)}, u32[]{:S(2)}, u32[]{:S(2)}) async-start(bf16[4,8,1024]{2,0,1:T(4,128)(2,1)} %copy.27), calls=%async_computation | async-start | bytes 131072 | tf_op jit(solution)/shard_map/all_to_all | solution.py:46
  43.9 0.7 copy-start.2
Sparse Core Ops, SparseCore 0:
  8.9 34.9 all-gather.2
where the time goes:
time: 177 us; the launch traced here: 174 us
  local copies, waits for them, and re-layouts  53.6 us (30%)
  other arithmetic  34.1 us (19%)
  matrix products  28.4 us (16%)
  blocking collectives  25.4 us (14%)
  between operations  13.5 us (8%)
  waiting for transfers between devices  12.7 us (7%)
  starting transfers between devices  5.2 us (3%)
    gather x16, local copies, waits for them, and re-layouts, one_tile(): near_f = jnp.take(all_f, index_row, axis=0)  29.9 us
    convert_element_type x16, other arithmetic, one_tile(): used = (slots < count).astype(jnp.float32)  21.5 us
    dot_general x16, matrix products, one_tile(): jnp.einsum('xq,kyq->kxy', own, near_f, preferred_element_type=jnp.float32)  17.1 us
    all_gather x1, blocking collectives, body(): lax.all_gather(local, 'ints', axis=1, tiled=True)  16.7 us
    select_n x16, other arithmetic, one_tile(): near_t = jnp.take(amp_tiles, index_row, axis=1)  11.1 us
    gather x16, local copies, waits for them, and re-layouts, one_tile(): near_t = jnp.take(amp_tiles, index_row, axis=1)  9.63 us
    dynamic_slice x16, local copies, waits for them, and re-layouts, tile_ladder(): stacked = lax.map(one_tile, (own_f, link_rows, count_rows))  9.38 us
    all_to_all x1, blocking collectives, body(): lax.all_to_all(rounded, 'pair', split_axis=0, concat_axis=1, tiled=True)  8.66 us
  transfers between devices with their start and end apart: 2, of which 2 were waited for; matrix products, arithmetic and copies ran while one was open for 1% of the time, Pallas kernels for 0%

commit v1 on v0

--- a/solution.py
+++ b/solution.py
@@ -1,7 +1,30 @@
+import functools
 import jax
 import jax.numpy as jnp
 from jax import lax
 from jax.sharding import PartitionSpec as P
+
+
+def chains_show(tile_in, comm_axis):
+    extra = lax.axis_size(comm_axis)
+    x_next = lax.axis_index(comm_axis)
+    local_now, tall, top = (extra, x_next, tile_in.shape[1])
+    parts_seen = [p * local_now if hop_no == 1 else p for hop_no, p in enumerate(tile_in.shape)]
+    next_value = jnp.zeros(parts_seen, tile_in.dtype)
+    mixed_arr = lax.dynamic_update_slice_in_dim(next_value, tile_in, tall * top, axis=1)
+    t = 1
+    while t < local_now:
+        tile_in = lax.ppermute(
+            tile_in, comm_axis, [(hop_no, (hop_no + 1) % local_now) for hop_no in range(local_now)]
+        )
+        mixed_arr = lax.dynamic_update_slice_in_dim(
+            mixed_arr, tile_in, (tall - t) % local_now * top, axis=1
+        )
+        t = t + 1
+    return mixed_arr
+
+
+packet_place = functools.partial(chains_show, comm_axis="ints")
 
 
 def split_high(values):
@@ -44,10 +67,7 @@
         pair_dev, nblocks, width
     )
     local = lax.all_to_all(masked, "pair", split_axis=1, concat_axis=0, tiled=True)[:, 0, :]
-    all_f, all_t = (
-        lax.all_gather(own_f, "ints", axis=0, tiled=True),
-        lax.all_gather(local, "ints", axis=1, tiled=True),
-    )
+    all_f, all_t = (lax.all_gather(own_f, "ints", axis=0, tiled=True), packet_place(local))
     result = tile_ladder(all_f, all_t, own_f, link_rows, count_rows)
     rounded = result.astype(jnp.bfloat16)[:, None, :]
     return lax.all_to_all(rounded, "pair", split_axis=0, concat_axis=1, tiled=True)

time: 177 us -> 176 us (level)
  blocking collectives: 25.4 us -> 7.69 us
  waiting for transfers between devices: 12.7 us -> 27.3 us
  starting transfers between devices: 5.2 us -> 7.74 us
    ppermute x0 -> x3, waiting for transfers between devices: none -> 19.9 us  [chains_show(): lax.ppermute(tile_in, comm_axis, [(hop_no, (hop_no + 1) % local_now) for...]
    all_gather x1 -> x0, blocking collectives: 16.7 us -> none  [body(): lax.all_gather(local, 'ints', axis=1, tiled=True)]
    all_gather x1, waiting for transfers between devices: 7.02 us -> 1.66 us  [body(): lax.all_gather(own_f, 'ints', axis=0, tiled=True)]
    ppermute x0 -> x3, starting transfers between devices: none -> 2.54 us  [chains_show(): lax.ppermute(tile_in, comm_axis, [(hop_no, (hop_no + 1) % local_now) for...]
  transfers between devices with their start and end apart: 2 -> 5, of which waited for: 2 -> 5; matrix products, arithmetic and copies ran while one was open for 1% -> 1% of each run, Pallas kernels for 0% -> 0%
where the time goes in v1:
time: 176 us; the launch traced here: 173 us
  local copies, waits for them, and re-layouts  53.7 us (31%)
  other arithmetic  34.1 us (19%)
  matrix products  28.4 us (16%)
  waiting for transfers between devices  27.3 us (16%)
  between operations  13.5 us (8%)
  starting transfers between devices  7.74 us (4%)
  blocking collectives  7.69 us (4%)
    gather x16, local copies, waits for them, and re-layouts, one_tile(): near_f = jnp.take(all_f, index_row, axis=0)  29.9 us
    convert_element_type x16, other arithmetic, one_tile(): used = (slots < count).astype(jnp.float32)  21.5 us
    ppermute x3, waiting for transfers between devices, chains_show(): lax.ppermute(tile_in, comm_axis, [(hop_no, (hop_no + 1) % local_now) for...  19.9 us
    dot_general x16, matrix products, one_tile(): jnp.einsum('xq,kyq->kxy', own, near_f, preferred_element_type=jnp.float32)  17.1 us
    select_n x16, other arithmetic, one_tile(): near_t = jnp.take(amp_tiles, index_row, axis=1)  11.1 us
    gather x16, local copies, waits for them, and re-layouts, one_tile(): near_t = jnp.take(amp_tiles, index_row, axis=1)  9.63 us
    dynamic_slice x16, local copies, waits for them, and re-layouts, tile_ladder(): stacked = lax.map(one_tile, (own_f, link_rows, count_rows))  9.38 us
    all_to_all x1, blocking collectives, body(): lax.all_to_all(rounded, 'pair', split_axis=0, concat_axis=1, tiled=True)  7.69 us
  transfers between devices with their start and end apart: 5, of which 5 were waited for; matrix products, arithmetic and copies ran while one was open for 1% of the time, Pallas kernels for 0%

profile of v1, /device:TPU:0, one launch (start us, length us, event | category | flops | bytes accessed | tf_op | source)
XLA Modules:
  0.0 173.2 jit_solution(7790041238544437167)
XLA Ops:
  6.5 0.7 all-gather.3.cloned.1.call-update
  9.0 5.2 %all-to-all-start = ((bf16[4,8,1024]{2,0,1:T(4,128)(2,1)}), bf16[4,8,1024]{2,0,1:T(4,128)(2,1)S(1)}, u32[]{:S(2)}, u32[]{:S(2)}) async-start(bf16[4,8,1024]{2,0,1:T(4,128)(2,1)} %copy.32), calls=%async_computation | async-start | bytes 131072 | tf_op jit(solution)/shard_map/all_to_all | solution.py:69
  14.2 5.0 %all-to-all-done = bf16[4,8,1024]{2,0,1:T(4,128)(2,1)S(1)} async-done(((bf16[4,8,1024]{2,0,1:T(4,128)(2,1)}), bf16[4,8,1024]{2,0,1:T(4,128)(2,1)S(1)}, u32[]{:S(2)}, u32[]{:S(2)}) %all-to-all-start) | async-done | bytes 65568 | tf_op jit(solution)/shard_map/all_to_all | solution.py:69
  19.2 1.6 collective-permute-start
  20.9 5.7 %collective-permute-done = bf16[32,1024]{1,0:T(8,128)(2,1)S(1)} collective-permute-done((bf16[32,1024]{1,0:T(8,128)(2,1)S(1)}, bf16[32,1024]{1,0:T(8,128)(2,1)S(1)}, u32[]{:S(2)}, u32[]{:S(2)}) %collective-permute-start) | collective-permute-done | bytes 65568 | tf_op jit(solution)/shard_map/ppermute | solution.py:17
  26.8 7.3 %collective-permute-done.1 = bf16[32,1024]{1,0:T(8,128)(2,1)S(1)} collective-permute-done((bf16[32,1024]{1,0:T(8,128)(2,1)S(1)}, bf16[32,1024]{1,0:T(8,128)(2,1)S(1)}, u32[]{:S(2)}, u32[]{:S(2)}) %collective-permute-start.1) | collective-permute-done | bytes 65568 | tf_op jit(solution)/shard_map/ppermute | solution.py:17
  34.1 0.7 collective-permute-start.2
  34.9 6.9 %collective-permute-done.2 = bf16[32,1024]{1,0:T(8,128)(2,1)S(1)} collective-permute-done((bf16[32,1024]{1,0:T(8,128)(2,1)S(1)}, bf16[32,1024]{1,0:T(8,128)(2,1)S(1)}, u32[]{:S(2)}, u32[]{:S(2)}) %collective-permute-start.2) | collective-permute-done | bytes 65568 | tf_op jit(solution)/shard_map/ppermute | solution.py:17
  42.6 1.7 all-gather.3.cloned.1.call-done
  45.0 110.9 %while.11 = (s32[]{:T(128)}, bf16[16,32,64]{2,1,0:T(8,128)(2,1)S(1)}, s32[16,32]{1,0:T(8,128)}, bf16[32,64,64]{2,0,1:T(8,128)(2,1)S(1)}, bf16[64,64,128]{2,1,0:T...) while((s32[]{:T(128)}, bf16[16,32,64]{2,1,0:T(8,128)(2,1)S(1)}, ...), condition=%wide.region_1.2_spmd.clone, body=%wide.region_0.1_spmd.clone.sunk | while | flops 51514720 | bytes 4389073 | solution.py:54
  45.5 1.3 compare_convert_fusion.2
  46.9 0.7 fusion.33
  47.6 1.9 %gather_fusion = bf16[32,64,128]{2,1,0:T(8,128)(2,1)S(1)} fusion(bf16[64,64,128]{2,1,0:T(8,128)(2,1)} %get-tuple-element.168, s32[1024]{0:T(1024)S(1)} %pad_clamp_fusion.2), kind=kCustom, calls=%fused_computation.1.clone.clone.1 | custom fusion | bytes 1048704 | tf_op jit(solution)/shard_map/while/body/eval_jaxpr/jit(_take)/gather | solution.py:44
  49.5 1.1 fusion.34
  52.5 1.3 compare_convert_fusion.2
  54.5 1.9 %gather_fusion = bf16[32,64,128]{2,1,0:T(8,128)(2,1)S(1)} fusion(bf16[64,64,128]{2,1,0:T(8,128)(2,1)} %get-tuple-element.168, s32[1024]{0:T(1024)S(1)} %pad_clamp_fusion.2), kind=kCustom, calls=%fused_computation.1.clone.clone.1 | custom fusion | bytes 1048704 | tf_op jit(solution)/shard_map/while/body/eval_jaxpr/jit(_take)/gather | solution.py:44
  56.4 1.1 fusion.34
  59.4 1.3 compare_convert_fusion.2
  61.4 1.9 %gather_fusion = bf16[32,64,128]{2,1,0:T(8,128)(2,1)S(1)} fusion(bf16[64,64,128]{2,1,0:T(8,128)(2,1)} %get-tuple-element.168, s32[1024]{0:T(1024)S(1)} %pad_clamp_fusion.2), kind=kCustom, calls=%fused_computation.1.clone.clone.1 | custom fusion | bytes 1048704 | tf_op jit(solution)/shard_map/while/body/eval_jaxpr/jit(_take)/gather | solution.py:44
  63.3 1.1 fusion.34
  66.3 1.3 compare_convert_fusion.2
  68.4 1.9 %gather_fusion = bf16[32,64,128]{2,1,0:T(8,128)(2,1)S(1)} fusion(bf16[64,64,128]{2,1,0:T(8,128)(2,1)} %get-tuple-element.168, s32[1024]{0:T(1024)S(1)} %pad_clamp_fusion.2), kind=kCustom, calls=%fused_computation.1.clone.clone.1 | custom fusion | bytes 1048704 | tf_op jit(solution)/shard_map/while/body/eval_jaxpr/jit(_take)/gather | solution.py:44
  70.2 1.1 fusion.34
  73.3 1.3 compare_convert_fusion.2
  74.6 0.7 fusion.33
  75.3 1.9 %gather_fusion = bf16[32,64,128]{2,1,0:T(8,128)(2,1)S(1)} fusion(bf16[64,64,128]{2,1,0:T(8,128)(2,1)} %get-tuple-element.168, s32[1024]{0:T(1024)S(1)} %pad_clamp_fusion.2), kind=kCustom, calls=%fused_computation.1.clone.clone.1 | custom fusion | bytes 1048704 | tf_op jit(solution)/shard_map/while/body/eval_jaxpr/jit(_take)/gather | solution.py:44
  77.2 1.1 fusion.34
  80.2 1.3 compare_convert_fusion.2
  82.2 1.9 %gather_fusion = bf16[32,64,128]{2,1,0:T(8,128)(2,1)S(1)} fusion(bf16[64,64,128]{2,1,0:T(8,128)(2,1)} %get-tuple-element.168, s32[1024]{0:T(1024)S(1)} %pad_clamp_fusion.2), kind=kCustom, calls=%fused_computation.1.clone.clone.1 | custom fusion | bytes 1048704 | tf_op jit(solution)/shard_map/while/body/eval_jaxpr/jit(_take)/gather | solution.py:44
  84.1 1.1 fusion.34
  87.1 1.3 compare_convert_fusion.2
  89.2 1.9 %gather_fusion = bf16[32,64,128]{2,1,0:T(8,128)(2,1)S(1)} fusion(bf16[64,64,128]{2,1,0:T(8,128)(2,1)} %get-tuple-element.168, s32[1024]{0:T(1024)S(1)} %pad_clamp_fusion.2), kind=kCustom, calls=%fused_computation.1.clone.clone.1 | custom fusion | bytes 1048704 | tf_op jit(solution)/shard_map/while/body/eval_jaxpr/jit(_take)/gather | solution.py:44
  91.0 1.1 fusion.34
  94.0 1.3 compare_convert_fusion.2
  95.4 0.7 fusion.33
  96.1 1.9 %gather_fusion = bf16[32,64,128]{2,1,0:T(8,128)(2,1)S(1)} fusion(bf16[64,64,128]{2,1,0:T(8,128)(2,1)} %get-tuple-element.168, s32[1024]{0:T(1024)S(1)} %pad_clamp_fusion.2), kind=kCustom, calls=%fused_computation.1.clone.clone.1 | custom fusion | bytes 1048704 | tf_op jit(solution)/shard_map/while/body/eval_jaxpr/jit(_take)/gather | solution.py:44
  98.0 1.1 fusion.34
  101.0 1.3 compare_convert_fusion.2
  102.3 0.7 fusion.33
  103.0 1.9 %gather_fusion = bf16[32,64,128]{2,1,0:T(8,128)(2,1)S(1)} fusion(bf16[64,64,128]{2,1,0:T(8,128)(2,1)} %get-tuple-element.168, s32[1024]{0:T(1024)S(1)} %pad_clamp_fusion.2), kind=kCustom, calls=%fused_computation.1.clone.clone.1 | custom fusion | bytes 1048704 | tf_op jit(solution)/shard_map/while/body/eval_jaxpr/jit(_take)/gather | solution.py:44
  104.9 1.1 fusion.34
  107.9 1.3 compare_convert_fusion.2
  110.0 1.9 %gather_fusion = bf16[32,64,128]{2,1,0:T(8,128)(2,1)S(1)} fusion(bf16[64,64,128]{2,1,0:T(8,128)(2,1)} %get-tuple-element.168, s32[1024]{0:T(1024)S(1)} %pad_clamp_fusion.2), kind=kCustom, calls=%fused_computation.1.clone.clone.1 | custom fusion | bytes 1048704 | tf_op jit(solution)/shard_map/while/body/eval_jaxpr/jit(_take)/gather | solution.py:44
  111.8 1.1 fusion.34
  114.8 1.3 compare_convert_fusion.2
  116.9 1.9 %gather_fusion = bf16[32,64,128]{2,1,0:T(8,128)(2,1)S(1)} fusion(bf16[64,64,128]{2,1,0:T(8,128)(2,1)} %get-tuple-element.168, s32[1024]{0:T(1024)S(1)} %pad_clamp_fusion.2), kind=kCustom, calls=%fused_computation.1.clone.clone.1 | custom fusion | bytes 1048704 | tf_op jit(solution)/shard_map/while/body/eval_jaxpr/jit(_take)/gather | solution.py:44
  118.8 1.1 fusion.34
  121.8 1.3 compare_convert_fusion.2
  123.8 1.9 %gather_fusion = bf16[32,64,128]{2,1,0:T(8,128)(2,1)S(1)} fusion(bf16[64,64,128]{2,1,0:T(8,128)(2,1)} %get-tuple-element.168, s32[1024]{0:T(1024)S(1)} %pad_clamp_fusion.2), kind=kCustom, calls=%fused_computation.1.clone.clone.1 | custom fusion | bytes 1048704 | tf_op jit(solution)/shard_map/while/body/eval_jaxpr/jit(_take)/gather | solution.py:44
  125.7 1.1 fusion.34
  128.7 1.3 compare_convert_fusion.2
  130.7 1.9 %gather_fusion = bf16[32,64,128]{2,1,0:T(8,128)(2,1)S(1)} fusion(bf16[64,64,128]{2,1,0:T(8,128)(2,1)} %get-tuple-element.168, s32[1024]{0:T(1024)S(1)} %pad_clamp_fusion.2), kind=kCustom, calls=%fused_computation.1.clone.clone.1 | custom fusion | bytes 1048704 | tf_op jit(solution)/shard_map/while/body/eval_jaxpr/jit(_take)/gather | solution.py:44
  132.6 1.1 fusion.34
  135.6 1.3 compare_convert_fusion.2
  137.7 1.9 %gather_fusion = bf16[32,64,128]{2,1,0:T(8,128)(2,1)S(1)} fusion(bf16[64,64,128]{2,1,0:T(8,128)(2,1)} %get-tuple-element.168, s32[1024]{0:T(1024)S(1)} %pad_clamp_fusion.2), kind=kCustom, calls=%fused_computation.1.clone.clone.1 | custom fusion | bytes 1048704 | tf_op jit(solution)/shard_map/while/body/eval_jaxpr/jit(_take)/gather | solution.py:44
  139.5 1.1 fusion.34
  142.6 1.3 compare_convert_fusion.2
  144.6 1.9 %gather_fusion = bf16[32,64,128]{2,1,0:T(8,128)(2,1)S(1)} fusion(bf16[64,64,128]{2,1,0:T(8,128)(2,1)} %get-tuple-element.168, s32[1024]{0:T(1024)S(1)} %pad_clamp_fusion.2), kind=kCustom, calls=%fused_computation.1.clone.clone.1 | custom fusion | bytes 1048704 | tf_op jit(solution)/shard_map/while/body/eval_jaxpr/jit(_take)/gather | solution.py:44
  146.5 1.1 fusion.34
  149.5 1.3 compare_convert_fusion.2
  151.5 1.9 %gather_fusion = bf16[32,64,128]{2,1,0:T(8,128)(2,1)S(1)} fusion(bf16[64,64,128]{2,1,0:T(8,128)(2,1)} %get-tuple-element.168, s32[1024]{0:T(1024)S(1)} %pad_clamp_fusion.2), kind=kCustom, calls=%fused_computation.1.clone.clone.1 | custom fusion | bytes 1048704 | tf_op jit(solution)/shard_map/while/body/eval_jaxpr/jit(_take)/gather | solution.py:44
  153.4 1.1 fusion.34
  156.5 1.0 reduce.1
  157.6 7.7 %all_to_all.33 = bf16[8,2,2048]{2,1,0:T(2,128)(2,1)S(1)} all-to-all(bf16[8,2,2048]{2,1,0:T(2,128)(2,1)S(1)} %reshape.86), channel_id=1, replica_groups=mesh['pair'=8,'ints'=4] {'pair'}, dimensions={0} | all-to-all | bytes 131072 | tf_op jit(solution)/shard_map/all_to_all | solution.py:73
  (122 shorter events, 44.1 us)
Async XLA Ops:
  6.5 37.8 %all-gather.3.cloned.1.call-start = ((), (), s32[]{:S(2)}) async-start(), calls=%async_computation.2 | async-start | bytes 1310720 | tf_op jit(solution)/shard_map/all_gather | solution.py:70
  6.5 0.7 copy-start.1
  7.4 0.8 copy-start
  9.0 10.2 %all-to-all-start = ((bf16[4,8,1024]{2,0,1:T(4,128)(2,1)}), bf16[4,8,1024]{2,0,1:T(4,128)(2,1)S(1)}, u32[]{:S(2)}, u32[]{:S(2)}) async-start(bf16[4,8,1024]{2,0,1:T(4,128)(2,1)} %copy.32), calls=%async_computation | async-start | bytes 131072 | tf_op jit(solution)/shard_map/all_to_all | solution.py:69
  19.2 7.4 %collective-permute-start = (bf16[32,1024]{1,0:T(8,128)(2,1)S(1)}, bf16[32,1024]{1,0:T(8,128)(2,1)S(1)}, u32[]{:S(2)}, u32[]{:S(2)}) collective-permute-start(bf16[32,1024]{1,0:T(8,128)(2,1)S(1)} %squeeze.27), channel_id=1, source_target_pairs={{0,1},{1,2},{2,3},{3,0},{4,5},{5,6},{6,7},{7,4},{8,9},{9,10},{10,1... | collective-permute-start | bytes 196616 | tf_op jit(solution)/shard_map/ppermute | solution.py:17
  26.6 7.5 %collective-permute-start.1 = (bf16[32,1024]{1,0:T(8,128)(2,1)S(1)}, bf16[32,1024]{1,0:T(8,128)(2,1)S(1)}, u32[]{:S(2)}, u32[]{:S(2)}) collective-permute-start(bf16[32,1024]{1,0:T(8,128)(2,1)S(1)} %collective-permute-done), channel_id=1, source_target_pairs={{0,1},{1,2},{2,3},{3,0},{4,5},{5,6},{6,7},{7,4},{8,9},{9,10},{10,1... | collective-permute-start | bytes 196616 | tf_op jit(solution)/shard_map/ppermute | solution.py:17
  34.1 7.6 %collective-permute-start.2 = (bf16[32,1024]{1,0:T(8,128)(2,1)S(1)}, bf16[32,1024]{1,0:T(8,128)(2,1)S(1)}, u32[]{:S(2)}, u32[]{:S(2)}) collective-permute-start(bf16[32,1024]{1,0:T(8,128)(2,1)S(1)} %collective-permute-done.1), channel_id=1, source_target_pairs={{0,1},{1,2},{2,3},{3,0},{4,5},{5,6},{6,7},{7,4},{8,9},{9,10},{10,1... | collective-permute-start | bytes 196616 | tf_op jit(solution)/shard_map/ppermute | solution.py:17
  44.3 0.7 copy-start.2
Sparse Core Ops, SparseCore 0:
  8.9 35.3 all-gather.2
